TPU v7x, 32 devices: a whole 2x2x4 slice. The times are simulated.
32 devices in a mesh: dp: 16 (over z, x, core), tp: 2 (over y).
Axes of the slice: x: 2, y: 2, z: 4, core: 2. Of those that a mesh axis runs over, the one named last changes fastest.
Arguments:
- layer_in: bfloat16 [16384, 768], P(('dp', 'tp')), may hold values from -6 to 6
- lengths: int32 [128, 17], P('dp'), may hold values from 0 to 77, as said below
- attn_gain: float32 [768], replicated, may hold values from 0.25 to 1.75
- attn_shift: float32 [768], replicated, may hold values from -2 to 2
- qkv_weight: bfloat16 [768, 3, 768], P(None, None, 'tp'), may hold values from -0.21875 to 0.21875
- qv_bias: float32 [2, 768], P(None, 'tp'), may hold values from -3 to 3
- out_weight: bfloat16 [768, 768], P('tp'), may hold values from -0.875 to 0.875
- out_bias: float32 [768], replicated, may hold values from -2 to 2
- mlp_gain: float32 [768], replicated, may hold values from 0.25 to 1.75
- mlp_shift: float32 [768], replicated, may hold values from -2 to 2
- up_weight: bfloat16 [768, 3072], P(None, 'tp'), may hold values from -0.21875 to 0.21875
- up_bias: float32 [3072], P('tp'), may hold values from -3 to 3
- down_weight: bfloat16 [3072, 768], P('tp'), may hold values from -0.15625 to 0.15625
- down_bias: float32 [768], replicated, may hold values from -2 to 2
- cotangent: bfloat16 [16384, 768], P(('dp', 'tp')), may hold values from -6 to 6
Outputs:
- layer_out: bfloat16 [16384, 768], P(('dp', 'tp'))
- in_grad: bfloat16 [16384, 768], P(('dp', 'tp'))
- attn_gain_grad: float32 [768], replicated
- attn_shift_grad: float32 [768], replicated
- qkv_weight_grad: float32 [768, 3, 768], P(None, None, 'tp')
- qv_bias_grad: float32 [2, 768], P(None, 'tp')
- out_weight_grad: float32 [768, 768], P('tp')
- out_bias_grad: float32 [768], replicated
- mlp_gain_grad: float32 [768], replicated
- mlp_shift_grad: float32 [768], replicated
- up_weight_grad: float32 [768, 3072], P(None, 'tp')
- up_bias_grad: float32 [3072], P('tp')
- down_weight_grad: float32 [3072, 768], P('tp')
- down_bias_grad: float32 [768], replicated
Inputs may be any that keep to these rules, and one draw needn't show every extreme that they name: Row r's captions take lengths[r, 0], lengths[r, 1], ... tokens in order from slot 0; each entry is 0 or between 8 and 77; after a 0 all entries of the row are 0; a row's entries sum to at most 128, and its slots from that sum on are padding.
All inputs are finite; a program needn't handle non-finite values.
Results may differ from a plain program's by a relative error of at most 0.017.
Values may be sent and summed in bfloat16 or wider, within the bound.
No kernel may reach another device: no remote copies, remote signals or barrier semaphores. Data moves between devices by JAX's collectives and lax.ppermute only.
A program may use at most 128 MiB of HBM per device.

v0:
```python
from functools import partial
import math
import jax
import jax.numpy as jnp
from jax import lax
from jax.sharding import PartitionSpec as P

HEAD = 64
SEQ = 128
norm_epsilon = 1e-05


def layer_norm(values, gain, shift):
    center = values - jnp.mean(values, axis=-1, keepdims=True)
    spread = jnp.mean(center * center, axis=-1, keepdims=True)
    return center * lax.rsqrt(spread + norm_epsilon) * gain + shift


def segment_masks(lengths):
    seg_ends = jnp.cumsum(lengths, axis=1)
    places = jnp.arange(SEQ, dtype=jnp.int32)
    segment = jnp.sum((seg_ends[:, None, :] <= places[None, :, None]).astype(jnp.int32), axis=2)
    tok_valid = places[None, :] < seg_ends[:, -1:]
    causal = places[None, :] <= places[:, None]
    self_pair = places[None, :] == places[:, None]
    same_seg = segment[:, :, None] == segment[:, None, :]
    allowed = same_seg & causal[None] & (tok_valid[:, None, :] | self_pair[None])
    return (allowed, tok_valid)


def on_device(
    layer_in,
    lengths,
    attn_gain,
    attn_shift,
    qkv_weight,
    qv_bias,
    out_weight,
    out_bias,
    mlp_gain,
    mlp_shift,
    up_weight,
    up_bias,
    down_weight,
    down_bias,
    cotangent,
):
    model_width = layer_in.shape[1]
    local_width = qkv_weight.shape[2]
    head_count = local_width // HEAD
    row_count = lengths.shape[0]
    tok_count = row_count * SEQ
    score_scale = 1.0 / math.sqrt(HEAD)
    allowed, tok_valid = segment_masks(lengths)
    valid_col = tok_valid.astype(jnp.float32)[:, :, None, None]
    valid_low = valid_col.astype(jnp.bfloat16)
    resid_in = layer_in.astype(jnp.float32)
    normed_attn = layer_norm(resid_in, attn_gain, attn_shift).astype(jnp.bfloat16)
    gathered_attn = lax.all_gather(normed_attn, "tp", axis=0, tiled=True)
    flat_qkv = qkv_weight.reshape(model_width, 3 * local_width)
    projected = jnp.dot(gathered_attn, flat_qkv, preferred_element_type=jnp.float32)
    queries = (projected[:, :local_width] + qv_bias[0]).astype(jnp.bfloat16)
    key_rows = projected[:, local_width : 2 * local_width].astype(jnp.bfloat16)
    value_rows = (projected[:, 2 * local_width :] + qv_bias[1]).astype(jnp.bfloat16)
    query_heads = queries.reshape(row_count, SEQ, head_count, HEAD)
    key_heads = key_rows.reshape(row_count, SEQ, head_count, HEAD)
    value_heads = value_rows.reshape(row_count, SEQ, head_count, HEAD)

    def scores_of():
        raw_scores = jnp.einsum(
            "rqhd,rkhd->rhqk", query_heads, key_heads, preferred_element_type=jnp.float32
        )
        return jnp.where(allowed[:, None], raw_scores * score_scale, -1e30)

    masked = scores_of()
    row_max = jnp.max(masked, axis=-1, keepdims=True)
    exp_scores = jnp.exp(masked - row_max)
    row_total = jnp.sum(exp_scores, axis=-1, keepdims=True)
    log_total = row_max + jnp.log(row_total)
    attn_probs = exp_scores / row_total
    probs_low = attn_probs.astype(jnp.bfloat16)
    attended = (
        jnp.einsum("rhqk,rkhd->rqhd", probs_low, value_heads, preferred_element_type=jnp.float32)
        * valid_col
    )
    attended_low = attended.reshape(tok_count, local_width).astype(jnp.bfloat16)
    row_piece = attended_low
    attn_sum = lax.psum_scatter(
        jnp.dot(row_piece, out_weight, preferred_element_type=jnp.float32).astype(jnp.bfloat16),
        "tp",
        scatter_dimension=0,
        tiled=True,
    ).astype(jnp.float32)
    resid_mid = resid_in + attn_sum + out_bias
    normed_mlp = layer_norm(resid_mid, mlp_gain, mlp_shift).astype(jnp.bfloat16)
    gathered_mlp = lax.all_gather(normed_mlp, "tp", axis=0, tiled=True)
    pre_act = jnp.dot(gathered_mlp, up_weight, preferred_element_type=jnp.float32) + up_bias
    activated = jax.nn.gelu(pre_act, approximate=False).astype(jnp.bfloat16)
    row_piece = activated
    mlp_sum = lax.psum_scatter(
        jnp.dot(row_piece, down_weight, preferred_element_type=jnp.float32).astype(jnp.bfloat16),
        "tp",
        scatter_dimension=0,
        tiled=True,
    ).astype(jnp.float32)
    layer_out = (resid_mid + mlp_sum + down_bias).astype(jnp.bfloat16)
    out_grad = cotangent.astype(jnp.float32)
    grad_rows = lax.all_gather(cotangent, "tp", axis=0, tiled=True)
    down_weight_grad = jnp.einsum(
        "tf,td->fd", activated, grad_rows, preferred_element_type=jnp.float32
    )
    act_grad = jnp.einsum("td,fd->tf", grad_rows, down_weight, preferred_element_type=jnp.float32)
    gelu_value, gelu_back = jax.vjp(partial(jax.nn.gelu, approximate=False), pre_act)
    pre_grad = gelu_back(act_grad)[0].astype(jnp.bfloat16)
    up_bias_grad = jnp.sum(pre_grad.astype(jnp.float32), axis=0)
    up_weight_grad = jnp.einsum(
        "td,tf->df", gathered_mlp, pre_grad, preferred_element_type=jnp.float32
    )
    row_piece = pre_grad
    normed_mlp_grad = lax.psum_scatter(
        jnp.einsum("tf,df->td", row_piece, up_weight, preferred_element_type=jnp.float32).astype(
            jnp.bfloat16
        ),
        "tp",
        scatter_dimension=0,
        tiled=True,
    ).astype(jnp.float32)
    norm_value, mlp_norm_back = jax.vjp(layer_norm, resid_mid, mlp_gain, mlp_shift)
    mid_part, mlp_gain_grad, mlp_shift_grad = mlp_norm_back(normed_mlp_grad)
    mid_grad = out_grad + mid_part
    down_bias_grad = jnp.sum(out_grad, axis=0)
    out_bias_grad = jnp.sum(mid_grad, axis=0)
    mid_low = mid_grad.astype(jnp.bfloat16)
    mid_rows = lax.all_gather(mid_low, "tp", axis=0, tiled=True)
    out_weight_grad = jnp.einsum(
        "te,td->ed", attended_low, mid_rows, preferred_element_type=jnp.float32
    )
    attended_grad = jnp.einsum(
        "td,ed->te", mid_rows, out_weight, preferred_element_type=jnp.float32
    )
    attended_grad = (
        attended_grad.astype(jnp.bfloat16).reshape(row_count, SEQ, head_count, HEAD) * valid_low
    )
    back_probs = jnp.exp(scores_of() - log_total)
    back_low = back_probs.astype(jnp.bfloat16)
    value_grad = jnp.einsum(
        "rhqk,rqhd->rkhd", back_low, attended_grad, preferred_element_type=jnp.float32
    )
    prob_grad = jnp.einsum(
        "rqhd,rkhd->rhqk", attended_grad, value_heads, preferred_element_type=jnp.float32
    )
    row_inner = jnp.sum(back_probs * prob_grad, axis=-1, keepdims=True)
    score_grad = (back_probs * (prob_grad - row_inner)).astype(jnp.bfloat16)
    query_grad = (
        jnp.einsum("rhqk,rkhd->rqhd", score_grad, key_heads, preferred_element_type=jnp.float32)
        * score_scale
    )
    key_grad = (
        jnp.einsum("rhqk,rqhd->rkhd", score_grad, query_heads, preferred_element_type=jnp.float32)
        * score_scale
    )
    query_low = query_grad.reshape(tok_count, local_width).astype(jnp.bfloat16)
    key_low = key_grad.reshape(tok_count, local_width).astype(jnp.bfloat16)
    value_low = value_grad.reshape(tok_count, local_width).astype(jnp.bfloat16)
    qkv_grad = jnp.concatenate([query_low, key_low, value_low], axis=1)
    qv_bias_grad = jnp.stack(
        [
            jnp.sum(query_low.astype(jnp.float32), axis=0),
            jnp.sum(value_low.astype(jnp.float32), axis=0),
        ]
    )
    qkv_weight_grad = jnp.einsum(
        "td,te->de", gathered_attn, qkv_grad, preferred_element_type=jnp.float32
    )
    qkv_weight_grad = qkv_weight_grad.reshape(model_width, 3, local_width)
    row_piece = qkv_grad
    normed_attn_grad = lax.psum_scatter(
        jnp.einsum("te,de->td", row_piece, flat_qkv, preferred_element_type=jnp.float32).astype(
            jnp.bfloat16
        ),
        "tp",
        scatter_dimension=0,
        tiled=True,
    ).astype(jnp.float32)
    attn_norm_value, attn_norm_back = jax.vjp(layer_norm, resid_in, attn_gain, attn_shift)
    in_part, attn_gain_grad, attn_shift_grad = attn_norm_back(normed_attn_grad)
    in_grad = (mid_grad + in_part).astype(jnp.bfloat16)
    (
        qkv_weight_grad,
        qv_bias_grad,
        out_weight_grad,
        up_weight_grad,
        up_bias_grad,
        down_weight_grad,
    ) = lax.psum(
        (
            qkv_weight_grad,
            qv_bias_grad,
            out_weight_grad,
            up_weight_grad,
            up_bias_grad,
            down_weight_grad,
        ),
        "dp",
    )
    (
        attn_gain_grad,
        attn_shift_grad,
        out_bias_grad,
        mlp_gain_grad,
        mlp_shift_grad,
        down_bias_grad,
    ) = lax.psum(
        (
            attn_gain_grad,
            attn_shift_grad,
            out_bias_grad,
            mlp_gain_grad,
            mlp_shift_grad,
            down_bias_grad,
        ),
        ("dp", "tp"),
    )
    return (
        layer_out,
        in_grad,
        attn_gain_grad,
        attn_shift_grad,
        qkv_weight_grad,
        qv_bias_grad,
        out_weight_grad,
        out_bias_grad,
        mlp_gain_grad,
        mlp_shift_grad,
        up_weight_grad,
        up_bias_grad,
        down_weight_grad,
        down_bias_grad,
    )


def solution(mesh):
    in_specs = (
        P(("dp", "tp"), None),
        P("dp", None),
        P(),
        P(),
        P(None, None, "tp"),
        P(None, "tp"),
        P("tp", None),
        P(),
        P(),
        P(),
        P(None, "tp"),
        P("tp"),
        P("tp", None),
        P(),
        P(("dp", "tp"), None),
    )
    out_specs = (
        P(("dp", "tp"), None),
        P(("dp", "tp"), None),
        P(),
        P(),
        P(None, None, "tp"),
        P(None, "tp"),
        P("tp", None),
        P(),
        P(),
        P(),
        P(None, "tp"),
        P("tp"),
        P("tp", None),
        P(),
    )
    return jax.shard_map(
        on_device, mesh=mesh, in_specs=in_specs, out_specs=out_specs, check_vma=False
    )
```

profile of v0, /device:TPU:0, one launch (start us, length us, event | category | flops | bytes accessed | tf_op | source)
XLA Modules:
  0.0 599.3 jit_solution(7558251490497962483)
XLA Ops:
  7.3 1.5 convert_reduce_fusion.3
  8.7 1.5 fusion.19
  10.2 2.4 fusion.17
  13.0 3.8 copy.64
  17.5 25.2 %all-gather.5.cloned.1.call-done = bf16[1024,768]{1,0:T(8,128)(2,1)} async-done(((bf16[512,768]{1,0:T(8,128)(2,1)}), bf16[1024,768]{1,0:T(8,128)(2,1)}) %all-gather.5.cloned.1.call-update) | async-done | bytes 1572880 | tf_op jit(solution)/shard_map/all_gather | solution.py:59
  42.7 4.2 fusion.59
  47.0 1.4 fusion.27
  48.4 2.3 copy.65
  50.7 2.2 copy.93
  54.1 2.2 copy.95
  56.3 1.4 copy.67
  57.9 2.2 fusion.58
  64.0 2.2 convolution_convert_fusion
  66.3 26.2 %reduce-scatter.5.cloned.1.call-done = bf16[512,768]{1,0:T(8,128)(2,1)} async-done(((bf16[1024,768]{1,0:T(8,128)(2,1)}), bf16[512,768]{1,0:T(8,128)(2,1)}) %reduce-scatter.5.cloned.1.call-update) | async-done | bytes 786448 | tf_op jit(solution)/shard_map/reduce_scatter | solution.py:88
  92.5 1.5 fusion.36
  94.0 1.6 multiply_reduce_fusion.1
  98.1 26.3 %all-gather.7.cloned.1.call-done = bf16[1024,768]{1,0:T(8,128)(2,1)} async-done(((bf16[512,768]{1,0:T(8,128)(2,1)}), bf16[1024,768]{1,0:T(8,128)(2,1)}) %all-gather.7.cloned.1.call-update) | async-done | bytes 1572880 | tf_op jit(solution)/shard_map/all_gather | solution.py:96
  124.4 7.4 %fusion.60 = f32[1024,1536]{1,0:T(8,128)} fusion(bf16[1024,768]{1,0:T(8,128)(2,1)} %all-gather.7.cloned.1.call-done, bf16[768,1536]{1,0:T(8,128)(2,1)} %param.25), kind=kOutput, calls=%fused_computation.128 | convolution fusion | flops 2415919104 | bytes 10223616 | tf_op jit(solution)/shard_map/dot_general | solution.py:97
  131.8 21.3 %all-gather.9.cloned.1.call-done = bf16[1024,768]{1,0:T(8,128)(2,1)} async-done(((bf16[512,768]{1,0:T(8,128)(2,1)}), bf16[1024,768]{1,0:T(8,128)(2,1)}) %all-gather.9.cloned.1.call-update) | async-done | bytes 1572880 | tf_op jit(solution)/shard_map/all_gather | solution.py:108
  153.1 19.3 %convert_reduce_fusion = (f32[1536]{0:T(1024)S(1)}, bf16[1024,1536]{1,0:T(8,128)(2,1)S(1)}, f32[1024,1536]{1,0:T(8,128)}) fusion(f32[1024,1536]{1,0:T(8,128)} %fusion.60, f32[1536]{0:T(1024)S(1)} %copy-done.25, bf16[1024,768]{1,0:T(8,128)(2,1)} %all-gather.9.cloned.1.call-done, bf16[1536,768]{1,0:T(8,128)(2,1)S(1)} %copy-done), kind=kOutput, calls=%fused_computation.2 | convolution fusion | flops 2533882368 | bytes 19673088 | tf_op jit(solution)/shard_map/td,fd->tf/dot_general | solution.py:112
  172.4 1.7 copy-done.12
  174.1 3.8 convolution_convert_fusion.2
  177.9 6.2 %multiply_convert_fusion = bf16[1024,1536]{1,0:T(8,128)(2,1)S(1)} fusion(f32[1024,1536]{1,0:T(8,128)} %get-tuple-element.66, f32[1024,1536]{1,0:T(8,128)} %fusion.60, f32[1536]{0:T(1024)S(1)} %copy-done.25), kind=kLoop, calls=%fused_computation.4 | loop fusion | flops 6291456 | bytes 15734784 | tf_op jit(solution)/shard_map/convert_element_type | solution.py:98
  184.2 1.7 copy-done.8
  185.8 3.7 convolution_convert_fusion.3
  189.6 14.6 %reduce-scatter.9.cloned.1.call-done = bf16[512,768]{1,0:T(8,128)(2,1)} async-done(((bf16[1024,768]{1,0:T(8,128)(2,1)}), bf16[512,768]{1,0:T(8,128)(2,1)}) %reduce-scatter.9.cloned.1.call-update) | async-done | bytes 786448 | tf_op jit(solution)/shard_map/reduce_scatter | solution.py:120
  204.1 2.2 convert_reduce_fusion.2
  207.5 24.8 %reduce-scatter.7.cloned.1.call-done = bf16[512,768]{1,0:T(8,128)(2,1)} async-done(((bf16[1024,768]{1,0:T(8,128)(2,1)}), bf16[512,768]{1,0:T(8,128)(2,1)}) %reduce-scatter.7.cloned.1.call-update) | async-done | bytes 786448 | tf_op jit(solution)/shard_map/reduce_scatter | solution.py:100
  232.3 3.7 fusion.57
  238.5 27.1 %all-gather.11.cloned.1.call-done = bf16[1024,768]{1,0:T(8,128)(2,1)} async-done(((bf16[512,768]{1,0:T(8,128)(2,1)}), bf16[1024,768]{1,0:T(8,128)(2,1)}) %all-gather.11.cloned.1.call-update) | async-done | bytes 1572880 | tf_op jit(solution)/shard_map/all_gather | solution.py:134
  265.6 3.4 convolution_convert_fusion.4
  269.0 2.3 copy.74
  271.3 1.5 copy.97
  282.0 3.5 convolution_convert_fusion.1
  285.9 7.4 %fusion.62 = f32[1536,768]{1,0:T(8,128)} fusion(bf16[1024,1536]{1,0:T(8,128)(2,1)} %copy-done.8, bf16[1024,768]{1,0:T(8,128)(2,1)} %all-gather.9.cloned.1.call-done), kind=kOutput, calls=%fused_computation.130 | convolution fusion | flops 2415919104 | bytes 9437184 | tf_op jit(solution)/shard_map/tf,td->fd/dot_general | solution.py:109
  293.3 4.4 fusion.61
  297.6 1.8 fusion.38
  300.2 3.8 fusion.63
  304.2 63.9 %all-reduce.1 = (f32[2,384]{1,0:T(2,128)}, f32[1536]{0:T(1024)}) all-reduce(f32[2,384]{1,0:T(2,128)S(1)} %pad_maximum_fusion, f32[1536]{0:T(1024)S(1)} %get-tuple-element.64), channel_id=1, replica_groups=mesh['dp'=16,'tp'=2] {'dp'}, use_global_device_ids=true, to_apply=%region_24.25 | all-reduce | flops 2304 | bytes 18432 | tf_op jit(solution)/shard_map/psum | solution.py:195
  368.1 1.8 convert_reduce_fusion.1
  369.9 2.1 fusion.23
  372.0 39.3 %all-reduce = (f32[768]{0:T(1024)}, f32[768]{0:T(1024)}, f32[768]{0:T(1024)}, f32[768]{0:T(1024)}, f32[768]{0:T(1024)}, /*index=5*/f32[768]{0:T(1024)}) all-reduce(f32[768]{0:T(1024)S(1)} %get-tuple-element.44, f32[768]{0:T(1024)S(1)} %get-tuple-element.48, ...), channel_id=1, replica_groups=mesh['dp'=16,'tp'=2] {'dp','tp'}, use_global_device_ids=true, to_apply=%region_18.19 | all-reduce | flops 4608 | bytes 36864 | tf_op jit(solution)/shard_map/psum | solution.py:213
  411.3 3.1 add_convert_fusion.1
  414.4 163.4 %all-reduce.5.cloned.1.call-done = (f32[768,3,384]{0,2,1:T(8,128)}, f32[384,768]{1,0:T(8,128)}, f32[768,1536]{1,0:T(8,128)}, f32[1536,768]{1,0:T(8,128)}) async-done(((f32[768,3,384]{0,2,1:T(8,128)}, f32[384,768]{1,0:T(8,128)}, f32[768,1536]{1,0:T(8,128)}, f32[1536,768]{1,0:T(8,128)}), (f32[768,3,384]{0,2,1:T(8,128)}, f32[384,768]{1,0:T(8,128)}, f32[768,1536]{1,0:T(8,128)}, ...) | async-done | bytes 14155792 | tf_op jit(solution)/shard_map/psum | solution.py:195
  577.8 5.2 copy.87
  582.9 2.5 copy.146
  585.4 4.9 copy.147
  590.3 2.2 copy.148
  (131 shorter events, 22.9 us)
Async XLA Ops:
  7.2 145.9 %copy-start = (bf16[1536,768]{1,0:T(8,128)(2,1)S(1)}, bf16[1536,768]{1,0:T(8,128)(2,1)}, u32[]{:S(2)}) copy-start(bf16[1536,768]{1,0:T(8,128)(2,1)} %param.27) | copy-start | bytes 7077892
  7.2 5.5 copy-start.27
  7.2 35.5 %all-gather.5.cloned.1.call-start = ((), (), s32[]{:S(2)}) async-start(), calls=%async_computation.4 | async-start | bytes 2359296 | tf_op jit(solution)/shard_map/all_gather | solution.py:59
  12.6 4.4 copy-start.29
  12.6 79.8 %reduce-scatter.5.cloned.1.call-start = ((), (), s32[]{:S(2)}) async-start(), calls=%async_computation.5 | async-start | bytes 2359296 | tf_op jit(solution)/shard_map/reduce_scatter | solution.py:88
  57.9 2.2 copy-start.10
  60.1 2.5 copy-start.2
  60.1 1.7 copy-start.14
  61.9 2.2 copy-start.33
  63.1 0.9 copy-start.18
  64.0 28.4 %copy-start.1 = (bf16[512,768]{1,0:T(8,128)(2,1)S(1)}, bf16[512,768]{1,0:T(8,128)(2,1)}, u32[]{:S(2)}) copy-start(bf16[512,768]{1,0:T(8,128)(2,1)} %param.15) | copy-start | bytes 2359300
  64.0 28.4 %copy-start.22 = (f32[768]{0:T(1024)S(1)}, f32[768]{0:T(1024)}, u32[]{:S(2)}) copy-start(f32[768]{0:T(1024)} %param.22) | copy-start | bytes 9220
  66.2 29.4 %copy-start.24 = (f32[768]{0:T(1024)S(1)}, f32[768]{0:T(1024)}, u32[]{:S(2)}) copy-start(f32[768]{0:T(1024)} %param.23) | copy-start | bytes 9220
  66.2 29.4 %copy-start.26 = (f32[768]{0:T(1024)S(1)}, f32[768]{0:T(1024)}, u32[]{:S(2)}) copy-start(f32[768]{0:T(1024)} %param.24) | copy-start | bytes 9220
  66.2 58.1 %all-gather.7.cloned.1.call-start = ((), (), s32[]{:S(2)}) async-start(), calls=%async_computation.6 | async-start | bytes 2359296 | tf_op jit(solution)/shard_map/all_gather | solution.py:96
  92.5 3.2 copy-start.4
  97.0 56.1 %all-gather.9.cloned.1.call-start = ((), (), s32[]{:S(2)}) async-start(), calls=%async_computation.8 | async-start | bytes 2359296 | tf_op jit(solution)/shard_map/all_gather | solution.py:108
  97.6 55.5 %copy-start.25 = (f32[1536]{0:T(1024)S(1)}, f32[1536]{0:T(1024)}, u32[]{:S(2)}) copy-start(f32[1536]{0:T(1024)} %param.26) | copy-start | bytes 18436
  97.6 106.5 %reduce-scatter.9.cloned.1.call-start = ((), (), s32[]{:S(2)}) async-start(), calls=%async_computation.9 | async-start | bytes 2359296 | tf_op jit(solution)/shard_map/reduce_scatter | solution.py:120
  153.1 21.0 %copy-start.30 = (bf16[768,1536]{1,0:T(8,128)(2,1)S(1)}, bf16[768,1536]{1,0:T(8,128)(2,1)}, u32[]{:S(2)}) copy-start(bf16[768,1536]{1,0:T(8,128)(2,1)} %param.25) | copy-start | bytes 7077892
  172.4 1.7 copy-start.12
  177.9 54.4 %reduce-scatter.7.cloned.1.call-start = ((), (), s32[]{:S(2)}) async-start(), calls=%async_computation.7 | async-start | bytes 2359296 | tf_op jit(solution)/shard_map/reduce_scatter | solution.py:100
  184.2 1.7 copy-start.8
  189.5 42.8 %copy-start.28 = (f32[768]{0:T(1024)S(1)}, f32[768]{0:T(1024)}, u32[]{:S(2)}) copy-start(f32[768]{0:T(1024)} %param.28) | copy-start | bytes 9220
  189.5 76.1 %all-gather.11.cloned.1.call-start = ((), (), s32[]{:S(2)}) async-start(), calls=%async_computation.10 | async-start | bytes 2359296 | tf_op jit(solution)/shard_map/all_gather | solution.py:134
  204.1 2.2 copy-start.5
  204.1 2.2 copy-start.7
  236.1 1.2 copy-start.6
  238.2 129.8 %reduce-scatter.11.cloned.1.call-start = ((), (), s32[]{:S(2)}) async-start(), calls=%async_computation.11 | async-start | bytes 2359296 | tf_op jit(solution)/shard_map/reduce_scatter | solution.py:177
  271.3 2.1 copy-start.3
  273.5 1.3 copy-start.15
  275.7 1.1 copy-start.11
  276.8 1.2 copy-start.9
  280.2 1.8 copy-start.16
  280.6 1.4 copy-start.20
  285.6 292.2 %all-reduce.5.cloned.1.call-start = ((), (), s32[]{:S(2)}) async-start(), calls=%async_computation.12 | async-start | bytes 28311552 | tf_op jit(solution)/shard_map/psum | solution.py:195
  285.9 7.4 %copy-start.13 = (bf16[1024,1536]{1,0:T(8,128)(2,1)S(1)}, bf16[1024,1536]{1,0:T(8,128)(2,1)}, u32[]{:S(2)}) copy-start(bf16[1024,1536]{1,0:T(8,128)(2,1)} %copy-done.12) | copy-start | bytes 9437188
  285.9 7.4 %copy-start.17 = (bf16[1024,768]{1,0:T(8,128)(2,1)S(1)}, bf16[1024,768]{1,0:T(8,128)(2,1)}, u32[]{:S(2)}) copy-start(bf16[1024,768]{1,0:T(8,128)(2,1)} %all-gather.7.cloned.1.call-done) | copy-start | bytes 4718596
  293.2 4.4 copy-start.19
  293.2 4.4 copy-start.32
  297.6 1.8 copy-start.21
  297.6 2.6 copy-start.31
  304.0 64.1 %copy-start.23 = (f32[768]{0:T(1024)S(1)}, f32[768]{0:T(1024)}, u32[]{:S(2)}) copy-start(f32[768]{0:T(1024)} %param.17) | copy-start | bytes 9220
  582.9 7.4 %slice-start = ((s8[4718592]{0:T(1024)(128)(4,1)}), s8[4194304]{0:T(1024)(128)(4,1)S(1)}, s32[]{:S(2)}) async-start(s8[4718592]{0:T(1024)(128)(4,1)} %bitcast.79), calls=%async_computation.13 | async-start | bytes 8388608
  585.4 4.9 slice-start.1
Sparse Core Ops, SparseCore 0:
  12.8 29.8 all-gather.4
  66.3 26.0 reduce-scatter.4
  97.1 27.2 all-gather.6
  125.8 27.2 all-gather.8
  178.0 26.0 reduce-scatter.8
  206.2 26.0 reduce-scatter.6
  238.4 27.2 all-gather.10
  285.7 26.0 reduce-scatter.10
  317.5 260.1 all-reduce.4
where the time goes:
time: 608 us; the launch traced here: 599 us
  waiting for transfers between devices  329 us (54%)
  blocking collectives  103 us (17%)
  matrix products  71.8 us (12%)
  local copies, waits for them, and re-layouts  44.1 us (7%)
  other arithmetic  35 us (6%)
  between operations  14.5 us (2%)
    psum x1, waiting for transfers between devices, on_device(): lax.psum((qkv_weight_grad, qv_bias_grad, out_weight_grad, up_weight_grad,...  163 us
    psum x1, blocking collectives, on_device(): lax.psum((qkv_weight_grad, qv_bias_grad, out_weight_grad, up_weight_grad,...  63.9 us
    psum x1, blocking collectives, on_device(): lax.psum((attn_gain_grad, attn_shift_grad, out_bias_grad, mlp_gain_grad,...  39.3 us
    unnamed x83, local copies, waits for them, and re-layouts  34.2 us
    all_gather x1, waiting for transfers between devices, on_device(): mid_rows = lax.all_gather(mid_low, 'tp', axis=0, tiled=True)  27.1 us
    all_gather x1, waiting for transfers between devices, on_device(): gathered_mlp = lax.all_gather(normed_mlp, 'tp', axis=0, tiled=True)  26.3 us
    reduce_scatter x1, waiting for transfers between devices, on_device(): lax.psum_scatter(jnp.dot(row_piece, out_weight, preferred_element_type=jn...  26.2 us
    all_gather x1, waiting for transfers between devices, on_device(): gathered_attn = lax.all_gather(normed_attn, 'tp', axis=0, tiled=True)  25.2 us
  transfers between devices with their start and end apart: 9, of which 8 were waited for; matrix products, arithmetic and copies ran while one was open for 8% of the time, Pallas kernels for 0%

commit v1 on v0

--- a/solution.py
+++ b/solution.py
@@ -203,6 +203,12 @@
         ),
         "dp",
     )
+
+    def seats_all_take(patch):
+        for dd in ("tp", "dp"):
+            patch = lax.psum(patch, dd)
+        return patch
+
     (
         attn_gain_grad,
         attn_shift_grad,
@@ -210,7 +216,7 @@
         mlp_gain_grad,
         mlp_shift_grad,
         down_bias_grad,
-    ) = lax.psum(
+    ) = seats_all_take(
         (
             attn_gain_grad,
             attn_shift_grad,
@@ -218,8 +224,7 @@
             mlp_gain_grad,
             mlp_shift_grad,
             down_bias_grad,
-        ),
-        ("dp", "tp"),
+        )
     )
     return (
         layer_out,

time: 608 us -> 607 us (level)
  blocking collectives: 103 us -> 70.6 us
  waiting for transfers between devices: 329 us -> 361 us
    psum x2, blocking collectives: 103 us -> 70.6 us  [seats_all_take(): patch = lax.psum(patch, dd)]
    psum x1, waiting for transfers between devices: 163 us -> 188 us  [on_device(): lax.psum((qkv_weight_grad, qv_bias_grad, out_weight_grad, up_weight_grad,...]
    reduce_scatter x1, waiting for transfers between devices: 0.01 us -> 7.63 us  [on_device(): lax.psum_scatter(jnp.einsum('te,de->td', row_piece, flat_qkv, preferred_e...]
  transfers between devices with their start and end apart: 9 -> 9, of which waited for: 8 -> 9; matrix products, arithmetic and copies ran while one was open for 8% -> 8% of each run, Pallas kernels for 0% -> 0%
where the time goes in v1:
time: 607 us; the launch traced here: 598 us
  waiting for transfers between devices  361 us (59%)
  matrix products  71.8 us (12%)
  blocking collectives  70.6 us (12%)
  local copies, waits for them, and re-layouts  44.1 us (7%)
  other arithmetic  34.8 us (6%)
  between operations  14.5 us (2%)
    psum x1, waiting for transfers between devices, on_device(): lax.psum((qkv_weight_grad, qv_bias_grad, out_weight_grad, up_weight_grad,...  188 us
    psum x2, blocking collectives, seats_all_take(): patch = lax.psum(patch, dd)  70.6 us
    unnamed x83, local copies, waits for them, and re-layouts  34.2 us
    all_gather x1, waiting for transfers between devices, on_device(): mid_rows = lax.all_gather(mid_low, 'tp', axis=0, tiled=True)  27.1 us
    all_gather x1, waiting for transfers between devices, on_device(): gathered_mlp = lax.all_gather(normed_mlp, 'tp', axis=0, tiled=True)  26.3 us
    reduce_scatter x1, waiting for transfers between devices, on_device(): lax.psum_scatter(jnp.dot(row_piece, out_weight, preferred_element_type=jn...  26.2 us
    all_gather x1, waiting for transfers between devices, on_device(): gathered_attn = lax.all_gather(normed_attn, 'tp', axis=0, tiled=True)  25.2 us
    reduce_scatter x1, waiting for transfers between devices, on_device(): lax.psum_scatter(jnp.dot(row_piece, down_weight, preferred_element_type=j...  24.9 us
  transfers between devices with their start and end apart: 9, of which 9 were waited for; matrix products, arithmetic and copies ran while one was open for 8% of the time, Pallas kernels for 0%

profile of v1, /device:TPU:0, one launch (start us, length us, event | category | flops | bytes accessed | tf_op | source)
XLA Modules:
  0.0 598.5 jit_solution(3915339775010583106)
XLA Ops:
  7.3 1.5 convert_reduce_fusion.3
  8.7 1.5 fusion.19
  10.2 2.4 fusion.17
  13.0 3.8 copy.64
  17.5 25.2 %all-gather.5.cloned.1.call-done = bf16[1024,768]{1,0:T(8,128)(2,1)} async-done(((bf16[512,768]{1,0:T(8,128)(2,1)}), bf16[1024,768]{1,0:T(8,128)(2,1)}) %all-gather.5.cloned.1.call-update) | async-done | bytes 1572880 | tf_op jit(solution)/shard_map/all_gather | solution.py:59
  42.7 4.2 fusion.59
  47.0 1.4 fusion.27
  48.4 2.3 copy.65
  50.7 2.2 copy.93
  54.1 2.2 copy.95
  57.9 2.2 fusion.58
  64.0 2.2 convolution_convert_fusion
  66.3 26.2 %reduce-scatter.5.cloned.1.call-done = bf16[512,768]{1,0:T(8,128)(2,1)} async-done(((bf16[1024,768]{1,0:T(8,128)(2,1)}), bf16[512,768]{1,0:T(8,128)(2,1)}) %reduce-scatter.5.cloned.1.call-update) | async-done | bytes 786448 | tf_op jit(solution)/shard_map/reduce_scatter | solution.py:88
  92.5 1.5 fusion.36
  94.0 1.6 multiply_reduce_fusion.1
  98.1 26.3 %all-gather.7.cloned.1.call-done = bf16[1024,768]{1,0:T(8,128)(2,1)} async-done(((bf16[512,768]{1,0:T(8,128)(2,1)}), bf16[1024,768]{1,0:T(8,128)(2,1)}) %all-gather.7.cloned.1.call-update) | async-done | bytes 1572880 | tf_op jit(solution)/shard_map/all_gather | solution.py:96
  124.4 7.4 %fusion.60 = f32[1024,1536]{1,0:T(8,128)} fusion(bf16[1024,768]{1,0:T(8,128)(2,1)} %all-gather.7.cloned.1.call-done, bf16[768,1536]{1,0:T(8,128)(2,1)} %param.25), kind=kOutput, calls=%fused_computation.128 | convolution fusion | flops 2415919104 | bytes 10223616 | tf_op jit(solution)/shard_map/dot_general | solution.py:97
  131.8 21.3 %all-gather.9.cloned.1.call-done = bf16[1024,768]{1,0:T(8,128)(2,1)} async-done(((bf16[512,768]{1,0:T(8,128)(2,1)}), bf16[1024,768]{1,0:T(8,128)(2,1)}) %all-gather.9.cloned.1.call-update) | async-done | bytes 1572880 | tf_op jit(solution)/shard_map/all_gather | solution.py:108
  153.1 19.3 %convert_reduce_fusion = (f32[1536]{0:T(1024)S(1)}, bf16[1024,1536]{1,0:T(8,128)(2,1)S(1)}, f32[1024,1536]{1,0:T(8,128)}) fusion(f32[1024,1536]{1,0:T(8,128)} %fusion.60, f32[1536]{0:T(1024)S(1)} %copy-done.25, bf16[1024,768]{1,0:T(8,128)(2,1)} %all-gather.9.cloned.1.call-done, bf16[1536,768]{1,0:T(8,128)(2,1)S(1)} %copy-done), kind=kOutput, calls=%fused_computation.2 | convolution fusion | flops 2533882368 | bytes 19673088 | tf_op jit(solution)/shard_map/td,fd->tf/dot_general | solution.py:112
  172.4 1.7 copy-done.12
  174.1 3.8 convolution_convert_fusion.2
  178.0 6.2 %multiply_convert_fusion = bf16[1024,1536]{1,0:T(8,128)(2,1)S(1)} fusion(f32[1024,1536]{1,0:T(8,128)} %get-tuple-element.72, f32[1024,1536]{1,0:T(8,128)} %fusion.60, f32[1536]{0:T(1024)S(1)} %copy-done.25), kind=kLoop, calls=%fused_computation.4 | loop fusion | flops 6291456 | bytes 15734784 | tf_op jit(solution)/shard_map/convert_element_type | solution.py:98
  184.2 1.7 copy-done.8
  185.8 3.7 convolution_convert_fusion.3
  189.6 14.6 %reduce-scatter.9.cloned.1.call-done = bf16[512,768]{1,0:T(8,128)(2,1)} async-done(((bf16[1024,768]{1,0:T(8,128)(2,1)}), bf16[512,768]{1,0:T(8,128)(2,1)}) %reduce-scatter.9.cloned.1.call-update) | async-done | bytes 786448 | tf_op jit(solution)/shard_map/reduce_scatter | solution.py:120
  204.1 2.2 convert_reduce_fusion.2
  207.5 24.9 %reduce-scatter.7.cloned.1.call-done = bf16[512,768]{1,0:T(8,128)(2,1)} async-done(((bf16[1024,768]{1,0:T(8,128)(2,1)}), bf16[512,768]{1,0:T(8,128)(2,1)}) %reduce-scatter.7.cloned.1.call-update) | async-done | bytes 786448 | tf_op jit(solution)/shard_map/reduce_scatter | solution.py:100
  232.4 3.7 fusion.57
  238.5 27.1 %all-gather.11.cloned.1.call-done = bf16[1024,768]{1,0:T(8,128)(2,1)} async-done(((bf16[512,768]{1,0:T(8,128)(2,1)}), bf16[1024,768]{1,0:T(8,128)(2,1)}) %all-gather.11.cloned.1.call-update) | async-done | bytes 1572880 | tf_op jit(solution)/shard_map/all_gather | solution.py:134
  265.6 3.4 convolution_convert_fusion.4
  269.0 2.3 copy.74
  271.4 1.5 copy.97
  282.1 3.5 convolution_convert_fusion.1
  285.9 7.4 %fusion.62 = f32[1536,768]{1,0:T(8,128)} fusion(bf16[1024,1536]{1,0:T(8,128)(2,1)} %copy-done.8, bf16[1024,768]{1,0:T(8,128)(2,1)} %all-gather.9.cloned.1.call-done), kind=kOutput, calls=%fused_computation.130 | convolution fusion | flops 2415919104 | bytes 9437184 | tf_op jit(solution)/shard_map/tf,td->fd/dot_general | solution.py:109
  293.3 4.4 fusion.61
  297.6 1.8 fusion.38
  300.2 3.8 fusion.63
  304.2 7.6 %reduce-scatter.11.cloned.1.call-done = bf16[512,768]{1,0:T(8,128)(2,1)} async-done(((bf16[1024,768]{1,0:T(8,128)(2,1)}), bf16[512,768]{1,0:T(8,128)(2,1)}) %reduce-scatter.11.cloned.1.call-update) | async-done | bytes 786448 | tf_op jit(solution)/shard_map/reduce_scatter | solution.py:177
  311.8 1.7 convert_reduce_fusion.1
  313.5 2.1 fusion.23
  315.6 7.1 %all-reduce.2 = (f32[768]{0:T(1024)S(1)}, f32[768]{0:T(1024)S(1)}, f32[768]{0:T(1024)S(1)}, f32[768]{0:T(1024)S(1)}, f32[768]{0:T(1024)S(1)}, /*index=5*/f32[768]{0:T(1024)S(1)}) all-reduce(f32[768]{0:T(1024)S(1)} %get-tuple-element.44, f32[768]{0:T(1024)S(1)} %get-tuple-element.48, ...), channel_id=1, replica_groups=mesh['dp'=16,'tp'=2] {'tp'}, use_global_device_ids=true, to_apply=%region_18.19 | all-reduce | flops 4608 | bytes 36864 | tf_op jit(solution)/shard_map/psum | solution.py:209
  322.7 63.5 %all-reduce = (f32[768]{0:T(1024)}, f32[768]{0:T(1024)}, f32[2,384]{1,0:T(2,128)}, f32[768]{0:T(1024)}, f32[768]{0:T(1024)}, /*index=5*/f32[768]{0:T(1024)}, f32[1536]{0:T(1024)}, f32[768]{0:T(1024)}) all-reduce(f32[768]{0:T(1024)S(1)} %get-tuple-element.64, f32[768]{0:T(1024)S(1)} %get-tuple-element.65, ...), channel_id=1, replica_groups=mesh['dp'=16,'tp'=2] {'dp'}, use_global_device_ids=true, to_apply=%region_19.20 | all-reduce | flops 6912 | bytes 55296 | tf_op jit(solution)/shard_map/psum | solution.py:209
  386.2 3.1 add_convert_fusion.1
  389.3 187.6 %all-reduce.5.cloned.1.call-done = (f32[768,3,384]{0,2,1:T(8,128)}, f32[384,768]{1,0:T(8,128)}, f32[768,1536]{1,0:T(8,128)}, f32[1536,768]{1,0:T(8,128)}) async-done(((f32[768,3,384]{0,2,1:T(8,128)}, f32[384,768]{1,0:T(8,128)}, f32[768,1536]{1,0:T(8,128)}, f32[1536,768]{1,0:T(8,128)}), (f32[768,3,384]{0,2,1:T(8,128)}, f32[384,768]{1,0:T(8,128)}, f32[768,1536]{1,0:T(8,128)}, ...) | async-done | bytes 14155792 | tf_op jit(solution)/shard_map/psum | solution.py:195
  576.9 5.2 copy.87
  582.1 2.5 copy.146
  584.6 4.9 copy.147
  589.5 2.2 copy.148
  (131 shorter events, 24.3 us)
Async XLA Ops:
  7.2 145.9 %copy-start = (bf16[1536,768]{1,0:T(8,128)(2,1)S(1)}, bf16[1536,768]{1,0:T(8,128)(2,1)}, u32[]{:S(2)}) copy-start(bf16[1536,768]{1,0:T(8,128)(2,1)} %param.27) | copy-start | bytes 7077892
  7.2 5.5 copy-start.27
  7.2 35.5 %all-gather.5.cloned.1.call-start = ((), (), s32[]{:S(2)}) async-start(), calls=%async_computation.4 | async-start | bytes 2359296 | tf_op jit(solution)/shard_map/all_gather | solution.py:59
  12.6 4.4 copy-start.29
  12.6 79.8 %reduce-scatter.5.cloned.1.call-start = ((), (), s32[]{:S(2)}) async-start(), calls=%async_computation.5 | async-start | bytes 2359296 | tf_op jit(solution)/shard_map/reduce_scatter | solution.py:88
  57.9 2.2 copy-start.10
  60.1 2.5 copy-start.2
  60.1 1.7 copy-start.14
  61.9 2.2 copy-start.33
  63.1 0.9 copy-start.18
  64.0 28.4 %copy-start.1 = (bf16[512,768]{1,0:T(8,128)(2,1)S(1)}, bf16[512,768]{1,0:T(8,128)(2,1)}, u32[]{:S(2)}) copy-start(bf16[512,768]{1,0:T(8,128)(2,1)} %param.15) | copy-start | bytes 2359300
  64.0 28.4 %copy-start.22 = (f32[768]{0:T(1024)S(1)}, f32[768]{0:T(1024)}, u32[]{:S(2)}) copy-start(f32[768]{0:T(1024)} %param.22) | copy-start | bytes 9220
  66.2 29.4 %copy-start.24 = (f32[768]{0:T(1024)S(1)}, f32[768]{0:T(1024)}, u32[]{:S(2)}) copy-start(f32[768]{0:T(1024)} %param.23) | copy-start | bytes 9220
  66.2 29.4 %copy-start.26 = (f32[768]{0:T(1024)S(1)}, f32[768]{0:T(1024)}, u32[]{:S(2)}) copy-start(f32[768]{0:T(1024)} %param.24) | copy-start | bytes 9220
  66.2 58.1 %all-gather.7.cloned.1.call-start = ((), (), s32[]{:S(2)}) async-start(), calls=%async_computation.6 | async-start | bytes 2359296 | tf_op jit(solution)/shard_map/all_gather | solution.py:96
  92.5 3.2 copy-start.4
  97.0 56.1 %all-gather.9.cloned.1.call-start = ((), (), s32[]{:S(2)}) async-start(), calls=%async_computation.8 | async-start | bytes 2359296 | tf_op jit(solution)/shard_map/all_gather | solution.py:108
  97.6 55.5 %copy-start.25 = (f32[1536]{0:T(1024)S(1)}, f32[1536]{0:T(1024)}, u32[]{:S(2)}) copy-start(f32[1536]{0:T(1024)} %param.26) | copy-start | bytes 18436
  97.6 106.5 %reduce-scatter.9.cloned.1.call-start = ((), (), s32[]{:S(2)}) async-start(), calls=%async_computation.9 | async-start | bytes 2359296 | tf_op jit(solution)/shard_map/reduce_scatter | solution.py:120
  153.1 21.0 %copy-start.30 = (bf16[768,1536]{1,0:T(8,128)(2,1)S(1)}, bf16[768,1536]{1,0:T(8,128)(2,1)}, u32[]{:S(2)}) copy-start(bf16[768,1536]{1,0:T(8,128)(2,1)} %param.25) | copy-start | bytes 7077892
  172.4 1.7 copy-start.12
  177.9 54.4 %reduce-scatter.7.cloned.1.call-start = ((), (), s32[]{:S(2)}) async-start(), calls=%async_computation.7 | async-start | bytes 2359296 | tf_op jit(solution)/shard_map/reduce_scatter | solution.py:100
  184.2 1.7 copy-start.8
  189.5 42.8 %copy-start.28 = (f32[768]{0:T(1024)S(1)}, f32[768]{0:T(1024)}, u32[]{:S(2)}) copy-start(f32[768]{0:T(1024)} %param.28) | copy-start | bytes 9220
  189.5 76.1 %all-gather.11.cloned.1.call-start = ((), (), s32[]{:S(2)}) async-start(), calls=%async_computation.10 | async-start | bytes 2359296 | tf_op jit(solution)/shard_map/all_gather | solution.py:134
  204.1 2.2 copy-start.5
  204.1 2.2 copy-start.7
  236.1 1.2 copy-start.6
  238.3 73.6 %reduce-scatter.11.cloned.1.call-start = ((), (), s32[]{:S(2)}) async-start(), calls=%async_computation.11 | async-start | bytes 2359296 | tf_op jit(solution)/shard_map/reduce_scatter | solution.py:177
  271.3 2.1 copy-start.3
  273.5 1.3 copy-start.15
  275.7 1.1 copy-start.11
  276.8 1.2 copy-start.9
  280.3 1.8 copy-start.16
  280.6 1.4 copy-start.20
  285.6 291.3 %all-reduce.5.cloned.1.call-start = ((), (), s32[]{:S(2)}) async-start(), calls=%async_computation.12 | async-start | bytes 28311552 | tf_op jit(solution)/shard_map/psum | solution.py:195
  285.9 7.4 %copy-start.13 = (bf16[1024,1536]{1,0:T(8,128)(2,1)S(1)}, bf16[1024,1536]{1,0:T(8,128)(2,1)}, u32[]{:S(2)}) copy-start(bf16[1024,1536]{1,0:T(8,128)(2,1)} %copy-done.12) | copy-start | bytes 9437188
  285.9 7.4 %copy-start.17 = (bf16[1024,768]{1,0:T(8,128)(2,1)S(1)}, bf16[1024,768]{1,0:T(8,128)(2,1)}, u32[]{:S(2)}) copy-start(bf16[1024,768]{1,0:T(8,128)(2,1)} %all-gather.7.cloned.1.call-done) | copy-start | bytes 4718596
  293.3 4.4 copy-start.19
  293.3 4.4 copy-start.32
  297.6 1.8 copy-start.21
  297.6 2.6 copy-start.31
  304.0 7.8 %copy-start.23 = (f32[768]{0:T(1024)S(1)}, f32[768]{0:T(1024)}, u32[]{:S(2)}) copy-start(f32[768]{0:T(1024)} %param.17) | copy-start | bytes 9220
  582.1 7.4 %slice-start = ((s8[4718592]{0:T(1024)(128)(4,1)}), s8[4194304]{0:T(1024)(128)(4,1)S(1)}, s32[]{:S(2)}) async-start(s8[4718592]{0:T(1024)(128)(4,1)} %bitcast.79), calls=%async_computation.13 | async-start | bytes 8388608
  584.6 4.9 slice-start.1
Sparse Core Ops, SparseCore 0:
  12.8 29.8 all-gather.4
  66.3 26.0 reduce-scatter.4
  97.1 27.2 all-gather.6
  125.8 27.2 all-gather.8
  178.0 26.0 reduce-scatter.8
  206.2 26.0 reduce-scatter.6
  238.4 27.2 all-gather.10
  285.7 26.0 reduce-scatter.10
  317.6 259.3 all-reduce.4
